TPU v7x, 1024 devices: a whole 4x4x32 slice. The times are simulated.
1024 devices in a mesh: gx: 8 (over y, core), gy: 32 (over z), lev: 4 (over x).
Axes of the slice: x: 4, y: 4, z: 32, core: 2. Of those that a mesh axis runs over, the one named last changes fastest.
Arguments:
- model_state: float32 [2, 16, 2048, 2048], P(None, 'lev', 'gy', 'gx'), as said below
- cutoff: int32 [2, 16], P(None, 'lev'), may hold values from 5 to 10, as said below
- relax_rate: float32 [2, 16], P(None, 'lev'), may hold values from 0.2 to 1
- owner_map: int32 [4, 2], P('lev'), may hold values from 0 to 255
- era_store: float32 [256, 2, 16, 882], P(('gx', 'gy'), None, 'lev'), may hold values from -0.36 to 0.36
Outputs:
- nudged: float32 [2, 16, 2048, 2048], P(None, 'lev', 'gy', 'gx')
Inputs may be any that keep to these rules, and one draw needn't show every extreme that they name: `cutoff`: each draw holds both the smallest and the largest value somewhere. `model_state`: finite values of order one.
All inputs are finite; a program needn't handle non-finite values.
Results may differ from a plain program's by a relative error of at most 0.00007.
Values sent between devices are 32-bit elements; how exact they have to be, the bound alone decides.
A program may use at most 32 MiB of HBM per device.

v0:
```python
import jax
import jax.numpy as jnp
from jax import lax
from jax.sharding import PartitionSpec as P

NX = 2048
NY = 2048
KC = 10
NK = 21


def from_root(value, axis, source):
    kept = jnp.where(lax.axis_index(axis) == source, value, 0).astype(value.dtype)
    return lax.psum(kept, axis)


def tables(positions, length):
    wave_index = jnp.arange(NK, dtype=jnp.int32) - KC
    turns = jnp.mod(positions[:, None] * wave_index[None, :], length).astype(jnp.float32)
    angle = turns * (6.2831855 / length)
    return (jnp.cos(angle), jnp.sin(angle))


def mix(form, left, right):
    return jnp.einsum(form, left, right, precision=lax.Precision.HIGHEST)


def forward_part(field, cos_y, sin_y, cos_x, sin_x):
    along_re = mix("vlyx,yk->vlkx", field, cos_y)
    along_im = -mix("vlyx,yk->vlkx", field, sin_y)
    part_re = mix("vlkx,xj->vlkj", along_re, cos_x) + mix("vlkx,xj->vlkj", along_im, sin_x)
    part_im = mix("vlkx,xj->vlkj", along_im, cos_x) - mix("vlkx,xj->vlkj", along_re, sin_x)
    return jnp.stack([part_re, part_im], axis=2) * (1.0 / (NX * NY))


def inverse_part(increment, cos_y, sin_y, cos_x, sin_x):
    delta_re = increment[:, :, 0]
    delta_im = increment[:, :, 1]
    back_re = mix("vlkj,xj->vlkx", delta_re, cos_x) - mix("vlkj,xj->vlkx", delta_im, sin_x)
    back_im = mix("vlkj,xj->vlkx", delta_re, sin_x) + mix("vlkj,xj->vlkx", delta_im, cos_x)
    return mix("vlkx,yk->vlyx", back_re, cos_y) - mix("vlkx,yk->vlyx", back_im, sin_y)


def body(model_state, cutoff, relax_rate, owner_map, era_store):
    nvar, levels, ny_local, nx_local = model_state.shape
    gx_pos = lax.axis_index("gx")
    gy_pos = lax.axis_index("gy")
    per_var = []
    for var_num in range(nvar):
        received = from_root(era_store, ("gx", "gy"), owner_map[0, var_num])
        per_var.append(received[0, var_num])
    analysis = jnp.stack(per_var).reshape(nvar, levels, 2, NK, NK)
    pencil = lax.all_to_all(model_state, "gy", split_axis=3, concat_axis=2, tiled=True)
    width = pencil.shape[3]
    y_pos = jnp.arange(NY, dtype=jnp.int32)
    x_pos = gx_pos * nx_local + gy_pos * width + jnp.arange(width, dtype=jnp.int32)
    cos_y, sin_y = tables(y_pos, NY)
    cos_x, sin_x = tables(x_pos, NX)
    partial_value = forward_part(pencil, cos_y, sin_y, cos_x, sin_x)
    spectrum = lax.psum(partial_value, ("gx", "gy"))
    wave_index = jnp.arange(NK, dtype=jnp.int32) - KC
    total_sq = wave_index[:, None] ** 2 + wave_index[None, :] ** 2
    keep = (total_sq[None, None] <= (cutoff**2)[:, :, None, None]).astype(jnp.float32)
    increment = relax_rate[:, :, None, None, None] * keep[:, :, None] * (analysis - spectrum)
    added = inverse_part(increment, cos_y, sin_y, cos_x, sin_x)
    return lax.all_to_all(pencil + added, "gy", split_axis=2, concat_axis=3, tiled=True)


def solution(mesh):
    placed = (
        P(None, "lev", "gy", "gx"),
        P(None, "lev"),
        P(None, "lev"),
        P("lev", None),
        P(("gx", "gy"), None, "lev", None),
    )
    return jax.shard_map(
        body, mesh=mesh, in_specs=placed, out_specs=P(None, "lev", "gy", "gx"), check_vma=False
    )
```

profile of v0, /device:TPU:1, one launch (start us, length us, event | category | flops | bytes accessed | tf_op | source)
XLA Modules:
  0.0 843.0 jit_solution(14420779098106511602)
XLA Ops:
  6.5 1.6 copy.14
  8.1 1.8 reshape.61
  9.9 29.3 %all-to-all-start = ((f32[32,1,4096]{2,1,0:T(1,128)}), f32[32,1,4096]{2,1,0:T(1,128)S(1)}, u32[]{:S(2)}, u32[]{:S(2)}) async-start(f32[32,1,4096]{2,1,0:T(1,128)} %reshape.61), calls=%async_computation | async-start | bytes 1048576 | tf_op jit(solution)/shard_map/all_to_all | solution.py:53
  39.2 0.8 integer_pow.18
  40.0 1.4 fusion.97
  42.7 1.4 broadcast_select_fusion.1
  44.1 59.3 %all-to-all-done = f32[32,1,4096]{2,1,0:T(1,128)S(1)} async-done(((f32[32,1,4096]{2,1,0:T(1,128)}), f32[32,1,4096]{2,1,0:T(1,128)S(1)}, u32[]{:S(2)}, u32[]{:S(2)}) %all-to-all-start) | async-done | bytes 524320 | tf_op jit(solution)/shard_map/all_to_all | solution.py:53
  104.0 1.8 reduce
  107.2 1.3 fusion.4
  108.6 1.3 convolution_bitcast_fusion
  111.5 0.7 maximum_multiply_fusion
  112.3 605.2 %all-reduce.3.cloned.1.call-done = (f32[2,4,2,21,21]{4,3,1,0,2:T(8,128)}, f32[1,2,4,882]{3,2,1,0:T(4,128)}, f32[1,2,4,882]{3,2,1,0:T(4,128)}) async-done(((f32[2,4,2,21,21]{4,3,1,0,2:T(8,128)}, f32[1,2,4,882]{3,2,1,0:T(4,128)}, f32[1,2,4,882]{3,2,1,0:T(4,128)}), (f32[2,4,2,21,21]{4,3,1,0,2:T(8,128)}, f32[1,2,4,882]{3,2,1,0:T(4,128)}, f32[1,2,4,882]{3,2,1,0:T(4,128)})) %all-reduce.3.cloned.1.call-update) | async-done | bytes 84688 | tf_op jit(solution)/shard_map/psum | solution.py:60
  717.5 0.7 slice.25
  718.2 0.7 slice.24
  719.2 1.0 fusion.13
  722.8 1.4 fusion.10
  724.2 1.4 fusion.1
  725.6 5.9 copy.19
  731.5 11.4 %reshape.63 = f32[32,1,4096]{2,1,0:T(1,128)S(1)} reshape(f32[2048,2,4,8]{3,2,1,0:T(4,128)} %bitcast.83) | data formatting | bytes 1048576
  743.0 72.9 %all_to_all.36 = f32[32,1,4096]{2,1,0:T(1,128)S(1)} all-to-all(f32[32,1,4096]{2,1,0:T(1,128)S(1)} %reshape.63), channel_id=1, replica_groups=mesh['gx'=8,'gy'=32,'lev'=4] {'gy'}, dimensions={0} | all-to-all | bytes 1048576 | tf_op jit(solution)/shard_map/all_to_all | solution.py:66
  815.9 1.8 reduce.1
  817.7 11.3 %reshape.64 = f32[2048,2,4,8]{3,2,1,0:T(4,128)} reshape(f32[32,4096]{1,0:T(8,128)S(1)} %reduce.1) | data formatting | bytes 1048576
  829.0 6.1 copy.20
  835.1 1.1 copy.21
  (24 shorter events, 6.7 us)
Async XLA Ops:
  6.5 105.7 %copy-start = (f32[2,4]{1,0:T(2,128)S(1)}, f32[2,4]{1,0:T(2,128)}, u32[]{:S(2)}) copy-start(f32[2,4]{1,0:T(2,128)} %param.7) | copy-start | bytes 100
  9.9 93.6 %all-to-all-start = ((f32[32,1,4096]{2,1,0:T(1,128)}), f32[32,1,4096]{2,1,0:T(1,128)S(1)}, u32[]{:S(2)}, u32[]{:S(2)}) async-start(f32[32,1,4096]{2,1,0:T(1,128)} %reshape.61), calls=%async_computation | async-start | bytes 1048576 | tf_op jit(solution)/shard_map/all_to_all | solution.py:53
  39.2 678.3 %all-reduce.3.cloned.1.call-start = ((), (), s32[]{:S(2)}) async-start(), calls=%async_computation.2 | async-start | bytes 507904 | tf_op jit(solution)/shard_map/psum | solution.py:60
Sparse Core Ops, SparseCore 0:
  112.4 605.0 all-reduce.2
where the time goes:
time: 844 us; the launch traced here: 843 us
  waiting for transfers between devices  664 us (79%)
  blocking collectives  72.9 us (9%)
  local copies, waits for them, and re-layouts  44.2 us (5%)
  starting transfers between devices  29.3 us (3%)
  between operations  14.9 us (2%)
  matrix products  9.66 us (1%)
    psum x1, waiting for transfers between devices, body(): spectrum = lax.psum(partial_value, ('gx', 'gy'))  605 us
    all_to_all x1, blocking collectives, body(): lax.all_to_all(pencil + added, 'gy', split_axis=2, concat_axis=3, tiled=T...  72.9 us
    all_to_all x1, waiting for transfers between devices, body(): lax.all_to_all(model_state, 'gy', split_axis=3, concat_axis=2, tiled=True)  59.3 us
    all_to_all x1, starting transfers between devices, body(): lax.all_to_all(model_state, 'gy', split_axis=3, concat_axis=2, tiled=True)  29.3 us
    unnamed x7, local copies, waits for them, and re-layouts  26.7 us
  transfers between devices with their start and end apart: 2, of which 2 were waited for; matrix products, arithmetic and copies ran while one was open for 0% of the time, Pallas kernels for 0%

commit v1 on v0

--- a/solution.py
+++ b/solution.py
@@ -7,11 +7,6 @@
 NY = 2048
 KC = 10
 NK = 21
-
-
-def from_root(value, axis, source):
-    kept = jnp.where(lax.axis_index(axis) == source, value, 0).astype(value.dtype)
-    return lax.psum(kept, axis)
 
 
 def tables(positions, length):
@@ -45,25 +40,20 @@
     nvar, levels, ny_local, nx_local = model_state.shape
     gx_pos = lax.axis_index("gx")
     gy_pos = lax.axis_index("gy")
-    per_var = []
-    for var_num in range(nvar):
-        received = from_root(era_store, ("gx", "gy"), owner_map[0, var_num])
-        per_var.append(received[0, var_num])
-    analysis = jnp.stack(per_var).reshape(nvar, levels, 2, NK, NK)
-    pencil = lax.all_to_all(model_state, "gy", split_axis=3, concat_axis=2, tiled=True)
-    width = pencil.shape[3]
-    y_pos = jnp.arange(NY, dtype=jnp.int32)
-    x_pos = gx_pos * nx_local + gy_pos * width + jnp.arange(width, dtype=jnp.int32)
+    me = gx_pos * lax.axis_size("gy") + gy_pos
+    y_pos = gy_pos * ny_local + jnp.arange(ny_local, dtype=jnp.int32)
+    x_pos = gx_pos * nx_local + jnp.arange(nx_local, dtype=jnp.int32)
     cos_y, sin_y = tables(y_pos, NY)
     cos_x, sin_x = tables(x_pos, NX)
-    partial_value = forward_part(pencil, cos_y, sin_y, cos_x, sin_x)
-    spectrum = lax.psum(partial_value, ("gx", "gy"))
+    mine = (owner_map[0] == me)[:, None, None]
+    kept = jnp.where(mine, era_store[0], 0.0).reshape(nvar, levels, 2, NK, NK)
+    share = kept - forward_part(model_state, cos_y, sin_y, cos_x, sin_x)
+    gap = lax.psum(share, ("gx", "gy"))
     wave_index = jnp.arange(NK, dtype=jnp.int32) - KC
     total_sq = wave_index[:, None] ** 2 + wave_index[None, :] ** 2
     keep = (total_sq[None, None] <= (cutoff**2)[:, :, None, None]).astype(jnp.float32)
-    increment = relax_rate[:, :, None, None, None] * keep[:, :, None] * (analysis - spectrum)
-    added = inverse_part(increment, cos_y, sin_y, cos_x, sin_x)
-    return lax.all_to_all(pencil + added, "gy", split_axis=2, concat_axis=3, tiled=True)
+    increment = relax_rate[:, :, None, None, None] * keep[:, :, None] * gap
+    return model_state + inverse_part(increment, cos_y, sin_y, cos_x, sin_x)
 
 
 def solution(mesh):

time: 844 us -> 1010 us (1.20)
  the two profiles are of different devices: /device:TPU:1 before, /device:TPU:2 now
where the time goes in v1:
time: 1010 us
  blocking collectives  999 us (99%)
    psum x1, blocking collectives, body(): gap = lax.psum(share, ('gx', 'gy'))  999 us

profile of v1, /device:TPU:2, one launch (start us, length us, event | category | flops | bytes accessed | tf_op | source)
XLA Modules:
  0.0 1009.9 jit_solution(10057003841170474854)
XLA Ops:
  0.0 0.6 copy-done.4
  0.7 0.0 copy-start.2
  0.7 0.7 copy-done.2
  1.4 0.1 broadcast_add_fusion
  1.4 0.6 copy-done.3
  2.0 0.1 compare_select_fusion
  2.1 0.0 copy-start
  2.1 1.6 fusion.2
  3.7 0.5 fusion.17
  4.2 0.5 convolution_bitcast_fusion
  4.7 0.5 fusion.3
  5.2 0.5 fusion.19
  5.7 0.0 copy-start.1
  5.7 0.5 fusion.4
  6.2 0.3 copy-done.1
  6.4 0.1 squeeze.10
  6.5 0.1 fusion.5
  6.6 999.0 %psum.7 = f32[2,4,2,21,21]{4,3,1,0,2:T(8,128)S(1)} all-reduce(f32[2,4,2,21,21]{4,3,1,0,2:T(8,128)S(1)} %fusion.5), channel_id=1, replica_groups=mesh['gx'=8,'gy'=32,'lev'=4] {'gx','gy'}, use_global_device_ids=true, to_apply=%region_0.1 | all-reduce | flops 7056 | bytes 56448 | tf_op jit(solution)/shard_map/psum | solution.py:51
  1005.6 0.5 fusion.6
  1006.1 0.5 convolution_add_fusion
  1006.6 0.5 fusion.7
  1007.1 0.5 convolution_subtract_fusion.1
  1007.6 0.8 fusion.26
  1008.3 1.6 fusion.1
  (10 shorter events, 0.0 us)
Async XLA Ops:
  0.0 0.7 copy-start.4
  0.7 0.7 copy-start.2
  1.4 0.7 copy-start.3
  2.1 2.1 copy-start
  5.7 0.8 copy-start.1

commit v2 on v1

v2 whole, which is shorter than its diff:
```python
import functools

import jax
import jax.numpy as jnp
import ml_dtypes
import numpy as np
from jax import lax
from jax.experimental import pallas as pl
from jax.experimental.pallas import tpu as pltpu
from jax.sharding import PartitionSpec as P

NX = 2048
NY = 2048
KC = 10
NK = 21
PAD = 24
WIDE = 32
LANES = 512
CHUNKS = LANES // 128
MESH = pl.DeviceIdType.MESH
BF16 = jnp.bfloat16
F32 = jnp.float32


def split(table):
    high = table.astype(ml_dtypes.bfloat16)
    low = (table - high.astype(np.float64)).astype(ml_dtypes.bfloat16)
    return np.stack([high, low])


def wavenumbers():
    return np.concatenate([np.arange(KC + 1), np.arange(1, KC + 1)])


def basis(length):
    wave = wavenumbers()
    angle = 2.0 * np.pi * np.mod(wave[:, None] * np.arange(length)[None, :], length) / length
    is_cos = (np.arange(NK) <= KC)[:, None]
    return np.where(is_cos, np.cos(angle), np.sin(angle))


def along_y_tables(n_gy, fields):
    ny = NY // n_gy
    out = np.zeros((n_gy, PAD, fields * ny))
    out[:, :NK] = np.tile(basis(NY).reshape(NK, n_gy, ny).transpose(1, 0, 2), (1, 1, fields))
    high, low = split(out)
    return np.stack([high, low], axis=1)


def along_x_tables(n_gx):
    nx = NX // n_gx
    out = np.zeros((n_gx, WIDE, nx))
    out[:, :NK] = basis(NX).reshape(NK, n_gx, nx).transpose(1, 0, 2)
    high, low = split(out)
    return np.stack([high, low], axis=1)


def pick_table():
    out = np.zeros((LANES, WIDE))
    p = np.arange(NK * NK)
    out[p, p % NK] = 1.0
    return out.astype(ml_dtypes.bfloat16)


def lane_tables():
    mask = np.zeros((PAD, LANES), np.float32)
    for a in range(NK):
        mask[a, a * NK : (a + 1) * NK] = 1.0
    wave = wavenumbers()
    twice = np.where(wave == 0, 1.0, 2.0)
    rows = np.zeros((16, LANES), np.float32)
    rows[:8, : NK * NK] = (np.outer(twice, twice) / (NX * NY)).reshape(-1)
    rows[8:] = 1e9
    rows[8:, : NK * NK] = (wave[:, None] ** 2 + wave[None, :] ** 2).reshape(-1)
    return mask, rows


def fold_table():
    wave = np.arange(NK) - KC
    number = wavenumbers()
    is_cos = np.arange(NK) <= KC
    hit = (number[:, None] == np.abs(wave)[None, :]).astype(np.float64)
    factor = np.where(is_cos[:, None], hit, hit * np.sign(wave)[None, :])
    both_cos = np.outer(is_cos, is_cos)
    both_sin = np.outer(~is_cos, ~is_cos)
    sign_re = both_cos.astype(np.float64) - both_sin.astype(np.float64)
    sign_im = -(~(both_cos | both_sin)).astype(np.float64)
    out = np.zeros((2, NK, NK, LANES))
    for part, sign in enumerate((sign_re, sign_im)):
        full = np.einsum("ak,bj,ab->kjab", factor, factor, sign)
        out[part, :, :, : NK * NK] = full.reshape(NK, NK, NK * NK)
    return out.reshape(2 * NK * NK, LANES).astype(ml_dtypes.bfloat16)


def halves(value):
    high = value.astype(BF16)
    low = (value - high.astype(F32)).astype(BF16)
    return high, low


def dot(left, right):
    return lax.dot_general(left, right, (((1,), (0,)), ((), ())), preferred_element_type=F32)


def dot_t(left, right):
    return lax.dot_general(left, right, (((1,), (1,)), ((), ())), preferred_element_type=F32)


def blocks(table):
    shape = (4 * PAD, table.shape[2])
    width = table.shape[2] // 4
    row = lax.broadcasted_iota(jnp.int32, shape, 0)
    lane = lax.broadcasted_iota(jnp.int32, shape, 1)
    keep = None
    for f in range(4):
        inside = (row >= f * PAD) & (row < (f + 1) * PAD) & (lane >= f * width) & (lane < (f + 1) * width)
        keep = inside if keep is None else keep | inside
    high, low = table[0].astype(F32), table[1].astype(F32)
    return (
        jnp.where(keep, jnp.concatenate([high] * 4, axis=0), 0.0),
        jnp.where(keep, jnp.concatenate([low] * 4, axis=0), 0.0),
    )


def along_y(block, table):
    high, low = halves(block)
    rows = table.shape[0] // 2
    both = dot(table, high)
    return both[:rows] + both[rows:] + dot(table[:rows], low)


def along_x(value, table, pick, mask):
    high, low = halves(value)
    narrow = dot_t(high, table[0]) + dot_t(high, table[1]) + dot_t(low, table[0])
    high, low = halves(narrow)
    wide = dot_t(high, pick) + dot_t(low, pick)
    return jnp.sum(wide.reshape(8, PAD, LANES) * mask[None], axis=1)


def folded(era, table):
    first = era.astype(BF16).astype(F32)
    rest = era - first
    second = rest.astype(BF16).astype(F32)
    third = rest - second
    out = dot(jnp.concatenate([first, second, third], axis=0).astype(BF16), table)
    return out[:8] + out[8:16] + out[16:24]


def back_x(coefs, table, mask):
    wide = (coefs[:, None, :] * mask[None]).reshape(8 * PAD, LANES)
    high, low = halves(wide)
    return dot(high, table[0]) + dot(high, table[1]) + dot(low, table[0])


def back_y(value, table):
    high, low = halves(value)
    return dot(table[0], high) + dot(table[0], low) + dot(table[1], high)


def kernel(
    n_y, n_z,
    cutoff, relax, owner, state, era, tab_y, tab_x, tab_pick, tab_fold, tab_mask, tab_rows,
    out,
    st, er, ty, tx, pick, fold, mask, rows, by, tx_wide, res, pay, got, got_y, mine_y, total,
    in_sem, out_sem, send_sem, recv_sem,
):
    gx = lax.axis_index("gx")
    gz = lax.axis_index("gy")
    y = gx // 2
    core = gx % 2
    is_root = jnp.logical_and(gz == 0, core == 0)
    is_second = jnp.logical_and(gz == 0, core == 1)
    half_z = n_z // 2

    def at(y_pos, z_pos, core_pos):
        return {"gx": y_pos * 2 + core_pos, "gy": z_pos}

    copies = [
        pltpu.make_async_copy(state.at[0], st.at[pl.ds(0, 4)], in_sem.at[0]),
        pltpu.make_async_copy(state.at[1], st.at[pl.ds(4, 4)], in_sem.at[1]),
        pltpu.make_async_copy(tab_y.at[gz], ty, in_sem.at[2]),
        pltpu.make_async_copy(tab_x.at[gx], tx, in_sem.at[3]),
        pltpu.make_async_copy(tab_mask, mask, in_sem.at[4]),
        pltpu.make_async_copy(era.at[0], er, in_sem.at[5]),
        pltpu.make_async_copy(tab_fold, fold, in_sem.at[6]),
        pltpu.make_async_copy(tab_rows, rows, in_sem.at[7]),
        pltpu.make_async_copy(tab_pick, pick, in_sem.at[8]),
    ]
    for copy in copies:
        copy.start()

    barrier = pltpu.get_barrier_semaphore()

    @pl.when(is_root)
    def _():
        def greet(i, carry):
            pl.semaphore_signal(barrier, inc=1, device_id=at(y, i // 2, i % 2), device_id_type=MESH)
            return carry

        lax.fori_loop(1, 2 * n_z, greet, 0)
        for step in range(1, n_y):
            pl.semaphore_signal(barrier, inc=1, device_id=at((y + step) % n_y, 0, 0), device_id_type=MESH)

    @pl.when(jnp.logical_not(is_root))
    def _():
        far = jnp.logical_and(core == 0, gz >= half_z)
        teller_z = jnp.where(core == 0, 0, gz)
        teller_core = jnp.where(far, 1, 0)
        pl.semaphore_signal(barrier, inc=1, device_id=at(y, teller_z, teller_core), device_id_type=MESH)

    copies[2].wait()
    y_high, y_low = blocks(ty[...])
    y_table = jnp.concatenate([y_high, y_low], axis=0).astype(BF16)
    copies[0].wait()
    low_fields = along_y(st[0:4].reshape(256, 256), y_table)
    copies[1].wait()
    high_fields = along_y(st[4:8].reshape(256, 256), y_table)
    copies[3].wait()
    copies[4].wait()
    copies[8].wait()
    partial = along_x(jnp.concatenate([low_fields, high_fields], axis=0), tx[...], pick[...], mask[...])
    copies[5].wait()
    copies[6].wait()
    held = folded(jnp.concatenate([er[0], er[1]], axis=0), fold[...])
    copies[7].wait()
    row = lax.broadcasted_iota(jnp.int32, (8, LANES), 0)
    me = gx * n_z + gz
    keeper = jnp.where(row < 4, owner[0, 0], owner[0, 1])
    share = jnp.where(keeper == me, held, 0.0) - rows[0:8] * partial
    for c in range(CHUNKS):
        pay[c] = share[:, c * 128 : (c + 1) * 128]

    def prepare():
        for part in range(2):
            tx_wide[part] = dot(pick[...], tx[part]).astype(BF16)
        by[0] = y_high.T.astype(BF16)
        by[1] = y_low.T.astype(BF16)

    rate = jnp.zeros((8, LANES), F32)
    limit = jnp.zeros((8, LANES), jnp.int32)
    for f in range(8):
        rate = jnp.where(row == f, relax[f // 4, f % 4], rate)
        limit = jnp.where(row == f, cutoff[f // 4, f % 4], limit)
    scale = jnp.where(rows[8:16] <= (limit * limit).astype(F32), rate, 0.0)

    def remote(src, dst, which, target):
        return pltpu.make_async_remote_copy(
            src, dst, send_sem.at[which], recv_sem.at[which], device_id=target, device_id_type=MESH
        )

    root = at(y, 0, 0)

    @pl.when(jnp.logical_not(is_root))
    def _():
        waits = jnp.where(is_second, 1 + n_z - half_z, jnp.where(core == 0, 2, 1))
        pl.semaphore_wait(barrier, waits)
        up = remote(pay, got.at[gz * 2 + core - 1], 0, root)
        up.start()
        prepare()
        remote(total, total, 2, root).wait_recv()

        @pl.when(is_second)
        def _():
            def tell(i, carry):
                remote(total, total, 2, at(y, n_z - 1 - i, 0)).start()
                return carry

            lax.fori_loop(0, n_z - half_z, tell, 0)

        @pl.when(jnp.logical_and(core == 0, gz > 0))
        def _():
            remote(total, total, 2, at(y, gz, 1)).start()

    @pl.when(is_root)
    def _():
        pl.semaphore_wait(barrier, half_z + n_y - 1)
        prepare()
        remote(got, got, 0, root).wait_recv()
        mine_y[...] = pay[...] + jnp.sum(got[...], axis=0)
        for step in range(1, n_y):
            remote(mine_y, got_y.at[step - 1], 1, at((y + step) % n_y, 0, 0)).start()
        remote(got_y, got_y, 1, root).wait_recv()
        total[...] = mine_y[...] + jnp.sum(got_y[...], axis=0)
        remote(total, total, 2, at(y, 0, 1)).start()

        def tell(i, carry):
            remote(total, total, 2, at(y, i, 0)).start()
            return carry

        lax.fori_loop(1, half_z, tell, 0)

    summed = jnp.concatenate([total[c] for c in range(CHUNKS)], axis=1)
    middle = back_x(summed * scale, tx_wide[...], mask[...])
    backs = []
    for h in range(2):
        added = back_y(middle[h * 4 * PAD : (h + 1) * 4 * PAD], by[...])
        res[4 * h : 4 * h + 4] = st[4 * h : 4 * h + 4] + added.reshape(4, 64, 256)
        back = pltpu.make_async_copy(res.at[pl.ds(4 * h, 4)], out.at[h], out_sem.at[h])
        back.start()
        backs.append(back)

    @pl.when(is_root)
    def _():
        remote(got_y, got_y, 1, root).wait_send()
        sent = got.at[pl.ds(0, half_z)]
        remote(sent, sent, 2, root).wait_send()

    @pl.when(jnp.logical_not(is_root))
    def _():
        remote(pay, pay, 0, root).wait_send()

    @pl.when(is_second)
    def _():
        sent = got.at[pl.ds(0, n_z - half_z)]
        remote(sent, sent, 2, root).wait_send()

    @pl.when(jnp.logical_and(core == 0, gz > 0))
    def _():
        remote(total, total, 2, root).wait_send()

    for back in backs:
        back.wait()


def solution(mesh):
    n_gx, n_gy = mesh.shape["gx"], mesh.shape["gy"]
    tables = (along_y_tables(n_gy, 4), along_x_tables(n_gx), pick_table(), fold_table(), *lane_tables())

    def body(model_state, cutoff, relax_rate, owner_map, era_store):
        smem = pl.BlockSpec(memory_space=pltpu.SMEM)
        anyw = pl.BlockSpec(memory_space=pl.ANY)
        vmem = pltpu.VMEM
        return pl.pallas_call(
            functools.partial(kernel, n_gx // 2, n_gy),
            out_shape=jax.ShapeDtypeStruct(model_state.shape, F32),
            in_specs=[smem] * 3 + [anyw] * 8,
            out_specs=anyw,
            scratch_shapes=[
                vmem((8, 64, 256), F32),
                vmem((2, 4, 2 * NK * NK), F32),
                vmem((2, PAD, 256), BF16),
                vmem((2, WIDE, 256), BF16),
                vmem((LANES, WIDE), BF16),
                vmem((2 * NK * NK, LANES), BF16),
                vmem((PAD, LANES), F32),
                vmem((16, LANES), F32),
                vmem((2, 256, 4 * PAD), BF16),
                vmem((2, LANES, 256), BF16),
                vmem((8, 64, 256), F32),
                vmem((CHUNKS, 8, 128), F32),
                vmem((2 * n_gy - 1, CHUNKS, 8, 128), F32),
                vmem((n_gx // 2 - 1, CHUNKS, 8, 128), F32),
                vmem((CHUNKS, 8, 128), F32),
                vmem((CHUNKS, 8, 128), F32),
                pltpu.SemaphoreType.DMA((9,)),
                pltpu.SemaphoreType.DMA((2,)),
                pltpu.SemaphoreType.DMA((3,)),
                pltpu.SemaphoreType.DMA((3,)),
            ],
            compiler_params=pltpu.CompilerParams(collective_id=0, has_side_effects=True),
        )(cutoff, relax_rate, owner_map, model_state, era_store, *(jnp.asarray(t) for t in tables))

    placed = (
        P(None, "lev", "gy", "gx"),
        P(None, "lev"),
        P(None, "lev"),
        P("lev", None),
        P(("gx", "gy"), None, "lev", None),
    )
    return jax.shard_map(
        body, mesh=mesh, in_specs=placed, out_specs=P(None, "lev", "gy", "gx"), check_vma=False
    )
```

time: 1010 us -> 46.2 us (0.05)
  the two profiles are of different devices: /device:TPU:2 before, /device:TPU:49 now
where the time goes in v2:
time: 46.2 us; the launch traced here: 46 us
  Pallas kernels  44.1 us (95%)
  local copies, waits for them, and re-layouts  1.87 us (4%)
    pallas_call x1, Pallas kernels, body(): pl.pallas_call(functools.partial(kernel, n_gx // 2, n_gy), out_shape=jax....  44.1 us
    unnamed x1, local copies, waits for them, and re-layouts  1.87 us

profile of v2, /device:TPU:49, one launch (start us, length us, event | category | flops | bytes accessed | tf_op | source)
XLA Modules:
  0.0 46.0 jit_solution(13507678839620589259)
XLA Ops:
  0.0 44.1 %shard_map.109 = f32[2,4,64,256]{3,2,1,0:T(8,128)} custom-call(s32[2,4]{1,0:T(2,128)} %cutoff.1, f32[2,4]{1,0:T(2,128)} %relax.1, s32[1,2]{1,0:T(1,128)} %owner.1, f32[2,4,64,256]{3,2,1,0:T(8,128)} %state.1, f32[1,2,4,882]{3,2,1,0:T(4,128)} %era.1, bf16[32,2,24,256]{3,2,1,0:T(8,128)(2,1)} %constant.12.clone.tab_y, ...), custom_call_target="tpu_custom_call" | custom-call | tf_op jit(solution)/shard_map/pallas_call | solution.py:333
  44.1 1.9 %copy.13 = f32[2,4,64,256]{3,2,1,0:T(8,128)} copy(f32[2,4,64,256]{3,2,1,0:T(8,128)} %shard_map.109) | data formatting | bytes 1048576

commit v3 on v2

v3 whole, which is shorter than its diff:
```python
import functools

import jax
import jax.numpy as jnp
import ml_dtypes
import numpy as np
from jax import lax
from jax.experimental import pallas as pl
from jax.experimental.pallas import tpu as pltpu
from jax.sharding import PartitionSpec as P

NX = 2048
NY = 2048
KC = 10
NK = 21
PAD = 24
WIDE = 32
FIELDS = 8
ROWS = NK * FIELDS
LANES = 512
CHUNKS = LANES // 128
FAR = (12, 20)
MESH = pl.DeviceIdType.MESH
BF16 = jnp.bfloat16
F32 = jnp.float32


def split(table):
    high = table.astype(ml_dtypes.bfloat16)
    low = (table - high.astype(np.float64)).astype(ml_dtypes.bfloat16)
    return np.stack([high, low])


def wavenumbers():
    return np.concatenate([np.arange(KC + 1), np.arange(1, KC + 1)])


def basis(length):
    wave = wavenumbers()
    angle = 2.0 * np.pi * np.mod(wave[:, None] * np.arange(length)[None, :], length) / length
    is_cos = (np.arange(NK) <= KC)[:, None]
    return np.where(is_cos, np.cos(angle), np.sin(angle))


def along_y_tables(n_gy, fields):
    ny = NY // n_gy
    out = np.zeros((n_gy, PAD, fields * ny))
    out[:, :NK] = np.tile(basis(NY).reshape(NK, n_gy, ny).transpose(1, 0, 2), (1, 1, fields))
    high, low = split(out)
    return np.stack([high, low], axis=1)


def along_x_tables(n_gx):
    nx = NX // n_gx
    out = np.zeros((n_gx, WIDE, nx))
    out[:, :NK] = basis(NX).reshape(NK, n_gx, nx).transpose(1, 0, 2)
    high, low = split(out)
    return np.stack([high, low], axis=1)


def pick_table():
    out = np.zeros((LANES, WIDE))
    p = np.arange(NK * NK)
    out[p, p % NK] = 1.0
    return out.astype(ml_dtypes.bfloat16)


def fold_tables():
    wave = np.arange(NK) - KC
    number = wavenumbers()
    is_cos = np.arange(NK) <= KC
    hit = (number[:, None] == np.abs(wave)[None, :]).astype(np.float64)
    factor = np.where(is_cos[:, None], hit, hit * np.sign(wave)[None, :])
    table = np.zeros((NK * NK, LANES))
    table[:, : NK * NK] = np.einsum("ak,bj->kjab", factor, factor).reshape(NK * NK, NK * NK)
    both_cos = np.outer(is_cos, is_cos)
    both_sin = np.outer(~is_cos, ~is_cos)
    twice = np.where(number == 0, 1.0, 2.0)
    kinds = [
        np.outer(twice, twice) / (NX * NY),
        number[:, None] ** 2 + number[None, :] ** 2,
        both_cos.astype(np.float64) - both_sin.astype(np.float64),
        -(~(both_cos | both_sin)).astype(np.float64),
    ]
    rows = np.zeros((4, FIELDS, LANES), np.float32)
    for kind, value in enumerate(kinds):
        rows[kind, :, : NK * NK] = value.reshape(-1)
    return table.astype(ml_dtypes.bfloat16), rows.reshape(4 * FIELDS, LANES)


def halves(value):
    high = value.astype(BF16)
    low = (value - high.astype(F32)).astype(BF16)
    return high, low


def dot(left, right):
    return lax.dot_general(left, right, (((1,), (0,)), ((), ())), preferred_element_type=F32)


def dot_t(left, right):
    return lax.dot_general(left, right, (((1,), (1,)), ((), ())), preferred_element_type=F32)


def blocks(table):
    shape = (FIELDS, 2 * table.shape[2])
    field = lax.broadcasted_iota(jnp.int32, shape, 0)
    lane = lax.broadcasted_iota(jnp.int32, shape, 1)
    width = shape[1] // FIELDS
    keep = (lane >= field * width) & (lane < (field + 1) * width)
    out = []
    for part in range(2):
        half = table[part].astype(F32)
        whole = jnp.concatenate([half, half], axis=1)[:NK]
        out.append(jnp.where(keep[None], whole[:, None, :], 0.0).reshape(ROWS, shape[1]))
    return out


def along_y(block, both_tables, high_table):
    high, low = halves(block)
    both = dot(both_tables, high)
    return both[:ROWS] + both[ROWS:] + dot(high_table, low)


def spans(a):
    return [
        (t, max(a * NK - 128 * t, 0), min((a + 1) * NK - 128 * t, 128))
        for t in range(a * NK // 128, (a * NK + NK - 1) // 128 + 1)
    ]


def along_x(value, table, pick):
    high, low = halves(value)
    narrow = dot_t(high, table[0]) + dot_t(high, table[1]) + dot_t(low, table[0])
    high, low = halves(narrow)
    wide = dot_t(high, pick) + dot_t(low, pick)
    lane = lax.broadcasted_iota(jnp.int32, (FIELDS, 128), 1)
    tiles = [None] * CHUNKS
    for a in range(NK):
        for t, start, _ in spans(a):
            here = wide[a * FIELDS : (a + 1) * FIELDS, t * 128 : (t + 1) * 128]
            tiles[t] = here if tiles[t] is None else jnp.where(lane >= start, here, tiles[t])
    return jnp.concatenate(tiles, axis=1)


def folded(era, table, sign_re, sign_im):
    parts = []
    for part in range(2):
        value = era[:, part * NK * NK : (part + 1) * NK * NK]
        first = value.astype(BF16).astype(F32)
        rest = value - first
        second = rest.astype(BF16).astype(F32)
        parts += [first, second, rest - second]
    out = dot(jnp.concatenate(parts, axis=0).astype(BF16), table)
    real = out[0:8] + out[8:16] + out[16:24]
    imag = out[24:32] + out[32:40] + out[40:48]
    return sign_re * real + sign_im * imag


def spread(coefs):
    lane = lax.broadcasted_iota(jnp.int32, (FIELDS, 128), 1)
    zero = jnp.zeros((FIELDS, 128), F32)
    rows = []
    for a in range(NK):
        tiles = [zero] * CHUNKS
        for t, start, stop in spans(a):
            tiles[t] = jnp.where((lane >= start) & (lane < stop), coefs[:, t * 128 : (t + 1) * 128], 0.0)
        rows.append(jnp.concatenate(tiles, axis=1))
    return jnp.concatenate(rows, axis=0)


def back_x(coefs, table):
    first = coefs.astype(BF16).astype(F32)
    high = spread(first)
    both = dot(jnp.concatenate([high, spread(coefs - first)], axis=0).astype(BF16), table[0])
    return both[:ROWS] + both[ROWS:] + dot(high.astype(BF16), table[1])


def back_y_tables(high, low):
    fill = jnp.zeros((512 - 3 * ROWS, high.shape[1]), F32)
    return jnp.concatenate([high, low, high, fill], axis=0).T.astype(BF16)


def back_y(value, table):
    high = value.astype(BF16).astype(F32)
    fill = jnp.zeros((512 - 3 * ROWS, value.shape[1]), F32)
    return dot(table, jnp.concatenate([high, high, value - high, fill], axis=0).astype(BF16))


def way_back():
    children = {
        (0, 0): [(0, 1), (1, 1), (4, 0), (1, 0), (3, 0), (2, 1), (2, 0), (8, 0)],
        (0, 1): [(31, 0)],
        (4, 0): [(5, 0), (5, 1), (6, 0), (7, 0), (6, 1), (4, 1)],
        (8, 0): [(8, 1), (12, 0), (9, 0), (10, 0), (11, 0)],
        (12, 0): [(12, 1), (13, 0), (14, 0), (15, 0)],
        (19, 0): [(19, 1), (16, 0), (17, 0), (18, 0)],
        (23, 0): [(23, 1), (20, 0), (21, 0), (22, 0)],
        (31, 0): [(31, 1), (19, 0), (23, 0)] + [(z, 0) for z in range(24, 31)],
    }
    parent = {child: node for node, nodes in children.items() for child in nodes}
    for z in range(1, 32):
        if (z, 1) not in parent:
            parent[z, 1] = (z, 0)
            children[z, 0] = [(z, 1)]
    return children, parent


def kernel(
    n_y, n_z,
    cutoff_in, relax_in, owner_in, state, era, tab_y, tab_x, tab_pick, tab_fold, tab_rows,
    out,
    cutoff, relax, owner, st, er, ty, tx, pick, fold, rows, by, tx_wide, scale, pay, got, got_y, mine_y, total,
    in_sem, send_sem, recv_sem,
):
    gx = lax.axis_index("gx")
    gz = lax.axis_index("gy")
    lev = lax.axis_index("lev")
    y = gx // 2
    children, parent = way_back()

    def swapped(y_pos):
        return jnp.where(jnp.logical_and(y_pos == 0, lev == 0), 1, 0)

    def at(y_pos, z_pos, slot):
        flip = swapped(y_pos)
        other = slot + flip - 2 * slot * flip
        return {"gx": y_pos * 2 + jnp.where(z_pos == 0, other, slot), "gy": z_pos}

    flip = swapped(y)
    core = gx % 2
    slot = jnp.where(gz == 0, core + flip - 2 * core * flip, core)
    index = 2 * gz + slot
    is_root = index == 0

    def by_index(table, default):
        value = jnp.int32(default)
        for key, entry in table.items():
            if entry != default:
                value = jnp.where(index == 2 * key[0] + key[1], entry, value)
        return value

    copies = [
        pltpu.make_async_copy(tab_y.at[gz], ty, in_sem.at[0]),
        pltpu.make_async_copy(state.at[0], st.at[pl.ds(0, 4)], in_sem.at[1]),
        pltpu.make_async_copy(state.at[1], st.at[pl.ds(4, 4)], in_sem.at[2]),
        pltpu.make_async_copy(tab_x.at[gx], tx, in_sem.at[3]),
        pltpu.make_async_copy(tab_pick, pick, in_sem.at[4]),
        pltpu.make_async_copy(era.at[0], er, in_sem.at[5]),
        pltpu.make_async_copy(tab_fold, fold, in_sem.at[6]),
        pltpu.make_async_copy(tab_rows, rows, in_sem.at[7]),
        pltpu.make_async_copy(owner_in, owner, in_sem.at[8]),
        pltpu.make_async_copy(cutoff_in, cutoff, in_sem.at[9]),
        pltpu.make_async_copy(relax_in, relax, in_sem.at[10]),
    ]
    for copy in copies:
        copy.start()

    barrier = pltpu.get_barrier_semaphore()

    @pl.when(is_root)
    def _():
        def greet(i, carry):
            pl.semaphore_signal(barrier, inc=1, device_id=at(y, i // 2, i % 2), device_id_type=MESH)
            return carry

        lax.fori_loop(1, 2 * n_z, greet, 0)
        for step in range(1, n_y):
            pl.semaphore_signal(barrier, inc=1, device_id=at((y + step) % n_y, 0, 0), device_id_type=MESH)

    @pl.when(jnp.logical_not(is_root))
    def _():
        parent_z = by_index({key: node[0] for key, node in parent.items() if node[0] != key[0]}, -1)
        parent_z = jnp.where(parent_z < 0, gz, parent_z)
        parent_slot = by_index({key: node[1] for key, node in parent.items()}, 0)
        pl.semaphore_signal(barrier, inc=1, device_id=at(y, parent_z, parent_slot), device_id_type=MESH)

    copies[0].wait()
    y_high, y_low = blocks(ty[...])
    y_both = jnp.concatenate([y_high, y_low], axis=0).astype(BF16)
    copies[1].wait()
    copies[2].wait()
    along = along_y(st[...].reshape(512, 256), y_both, y_high.astype(BF16))
    copies[3].wait()
    copies[4].wait()
    partial = along_x(along, tx[...], pick[...])
    for copy in copies[5:]:
        copy.wait()
    held = folded(jnp.concatenate([er[0], er[1]], axis=0), fold[...], rows[16:24], rows[24:32])
    row = lax.broadcasted_iota(jnp.int32, (8, LANES), 0)
    me = gx * n_z + gz
    keeper = jnp.where(row < 4, owner[0, 0], owner[0, 1])
    share = jnp.where(keeper == me, held, 0.0) - rows[0:8] * partial
    for c in range(CHUNKS):
        pay[c] = share[:, c * 128 : (c + 1) * 128]

    def prepare():
        rate = jnp.zeros((8, LANES), F32)
        limit = jnp.zeros((8, LANES), jnp.int32)
        for f in range(8):
            rate = jnp.where(row == f, relax[f // 4, f % 4], rate)
            limit = jnp.where(row == f, cutoff[f // 4, f % 4], limit)
        scale[...] = jnp.where(rows[8:16] <= (limit * limit).astype(F32), rate, 0.0)
        for part in range(2):
            tx_wide[part] = dot(pick[...], tx[part]).astype(BF16)
        by[...] = back_y_tables(y_high, y_low)

    n_far = 2 * (FAR[1] - FAR[0])
    n_near = 2 * n_z - 1 - n_far

    def remote(src, dst, which, target):
        return pltpu.make_async_remote_copy(
            src, dst, send_sem.at[which % 3], recv_sem.at[which], device_id=target, device_id_type=MESH
        )

    root = at(y, 0, 0)
    busy = [key for key, nodes in children.items() if key == (0, 1) or len(nodes) > 1]
    is_relay = jnp.logical_and(slot == 0, by_index({key: len(nodes) for key, nodes in children.items()}, 0) == 1)

    def pass_on(key):
        for z, child_slot in children[key]:
            remote(total, total, 2, at(y, z, child_slot)).start()

    @pl.when(jnp.logical_not(is_root))
    def _():
        pl.semaphore_wait(barrier, 1 + by_index({key: len(nodes) for key, nodes in children.items()}, 0))
        far = jnp.logical_and(gz >= FAR[0], gz < FAR[1])
        after = jnp.where(gz >= FAR[1], index - 2 * (FAR[1] - FAR[0]), index)
        place = jnp.where(far, n_near + index - 2 * FAR[0], after - 1)
        pltpu.make_async_remote_copy(
            pay, got.at[place], send_sem.at[0], recv_sem.at[jnp.where(far, 3, 0)],
            device_id=root, device_id_type=MESH,
        ).start()
        prepare()
        remote(total, total, 2, root).wait_recv()

    for key in busy:
        if key != (0, 0):
            pl.when(index == 2 * key[0] + key[1])(functools.partial(pass_on, key))

    @pl.when(is_relay)
    def _():
        remote(total, total, 2, at(y, gz, 1)).start()

    @pl.when(is_root)
    def _():
        pl.semaphore_wait(barrier, len(children[0, 0]) + n_y - 1)
        prepare()
        near, far = got.at[pl.ds(0, n_near)], got.at[pl.ds(n_near, n_far)]
        remote(near, near, 0, root).wait_recv()
        first = pay[...] + jnp.sum(near[...], axis=0)
        remote(far, far, 3, root).wait_recv()
        mine_y[...] = first + jnp.sum(far[...], axis=0)
        for step in range(1, n_y):
            remote(mine_y, got_y.at[step - 1], 1, at((y + step) % n_y, 0, 0)).start()
        remote(got_y, got_y, 1, root).wait_recv()
        total[...] = mine_y[...] + jnp.sum(got_y[...], axis=0)
        pass_on((0, 0))

    summed = jnp.concatenate([total[c] for c in range(CHUNKS)], axis=1)
    added = back_y(back_x(summed * scale[...], tx_wide[...]), by[...])
    for h in range(2):
        block = added[256 * h : 256 * (h + 1)].reshape(4, 64, 256)
        out[h] = st[4 * h : 4 * h + 4] + block

    def pass_on_sent(count):
        sent = got.at[pl.ds(0, count)]
        remote(sent, sent, 2, root).wait_send()

    @pl.when(is_root)
    def _():
        remote(got_y, got_y, 1, root).wait_send()

    @pl.when(jnp.logical_not(is_root))
    def _():
        remote(pay, pay, 0, root).wait_send()

    for key in busy:
        pl.when(index == 2 * key[0] + key[1])(functools.partial(pass_on_sent, len(children[key])))

    @pl.when(is_relay)
    def _():
        pass_on_sent(1)


def solution(mesh):
    n_gx, n_gy = mesh.shape["gx"], mesh.shape["gy"]
    tables = (along_y_tables(n_gy, FIELDS // 2), along_x_tables(n_gx), pick_table(), *fold_tables())

    def body(model_state, cutoff, relax_rate, owner_map, era_store):
        arrays = (cutoff, relax_rate, owner_map, model_state, era_store, *(jnp.asarray(t) for t in tables))
        vmem = pltpu.VMEM
        return pl.pallas_call(
            functools.partial(kernel, n_gx // 2, n_gy),
            out_shape=jax.ShapeDtypeStruct(model_state.shape, F32),
            in_specs=[pl.BlockSpec(memory_space=pltpu.HBM)] * 10,
            out_specs=pl.BlockSpec(memory_space=vmem),
            scratch_shapes=[
                pltpu.SMEM((2, 4), jnp.int32),
                pltpu.SMEM((2, 4), F32),
                pltpu.SMEM((1, 2), jnp.int32),
                vmem((8, 64, 256), F32),
                vmem((2, 4, 2 * NK * NK), F32),
                vmem((2, PAD, 256), BF16),
                vmem((2, WIDE, 256), BF16),
                vmem((LANES, WIDE), BF16),
                vmem((NK * NK, LANES), BF16),
                vmem((4 * FIELDS, LANES), F32),
                vmem((512, 512), BF16),
                vmem((2, LANES, 256), BF16),
                vmem((8, LANES), F32),
                vmem((CHUNKS, 8, 128), F32),
                vmem((2 * n_gy - 1, CHUNKS, 8, 128), F32),
                vmem((n_gx // 2 - 1, CHUNKS, 8, 128), F32),
                vmem((CHUNKS, 8, 128), F32),
                vmem((CHUNKS, 8, 128), F32),
                pltpu.SemaphoreType.DMA((11,)),
                pltpu.SemaphoreType.DMA((3,)),
                pltpu.SemaphoreType.DMA((4,)),
            ],
            compiler_params=pltpu.CompilerParams(
                collective_id=0, has_side_effects=True, vmem_limit_bytes=16 << 20
            ),
        )(*(pltpu.with_memory_space_constraint(array, pltpu.HBM) for array in arrays))

    placed = (
        P(None, "lev", "gy", "gx"),
        P(None, "lev"),
        P(None, "lev"),
        P("lev", None),
        P(("gx", "gy"), None, "lev", None),
    )
    return jax.shard_map(
        body, mesh=mesh, in_specs=placed, out_specs=P(None, "lev", "gy", "gx"), check_vma=False
    )
```

time: 46.2 us -> 42.1 us (0.911)
  the two profiles are of different devices: /device:TPU:49 before, /device:TPU:229 now
where the time goes in v3:
time: 42.1 us; the launch traced here: 41.9 us
  Pallas kernels  41.1 us (98%)
  local copies, waits for them, and re-layouts  0.8 us (2%)
    pallas_call x1, Pallas kernels, body(): pl.pallas_call(functools.partial(kernel, n_gx // 2, n_gy), out_shape=jax....  41.1 us

profile of v3, /device:TPU:229, one launch (start us, length us, event | category | flops | bytes accessed | tf_op | source)
XLA Modules:
  0.0 41.9 jit_solution(11130469416821846742)
XLA Ops:
  0.0 41.1 %shard_map.100 = f32[2,4,64,256]{3,2,1,0:T(8,128)S(1)} custom-call(s32[2,4]{1,0:T(2,128)} %cutoff_in.1, f32[2,4]{1,0:T(2,128)} %relax_in.1, s32[1,2]{1,0:T(1,128)} %owner_in.1, f32[2,4,64,256]{3,2,1,0:T(8,128)} %state.1, f32[1,2,4,882]{3,2,1,0:T(4,128)} %era.1, bf16[32,2,24,256]{3,2,1,0:T(8,128)(2,1)} %constant.10.clone.tab_y, ...), custom_call_target="tpu_custom_call" | custom-call | tf_op jit(solution)/shard_map/pallas_call | solution.py:393
  41.1 0.8 %copy.12 = f32[2,4,64,256]{3,2,1,0:T(8,128)} copy(f32[2,4,64,256]{3,2,1,0:T(8,128)S(1)} %shard_map.100) | data formatting | bytes 1048576

commit v4 on v3

--- a/solution.py
+++ b/solution.py
@@ -19,6 +19,7 @@
 ROWS = NK * FIELDS
 LANES = 512
 CHUNKS = LANES // 128
+ROOTS = (0, 8)
 FAR = (12, 20)
 MESH = pl.DeviceIdType.MESH
 BF16 = jnp.bfloat16
@@ -59,9 +60,9 @@
 
 
 def pick_table():
-    out = np.zeros((LANES, WIDE))
+    out = np.zeros((WIDE, LANES))
     p = np.arange(NK * NK)
-    out[p, p % NK] = 1.0
+    out[p % NK, p] = 1.0
     return out.astype(ml_dtypes.bfloat16)
 
 
@@ -116,6 +117,10 @@
     return out
 
 
+def dot_0(left, right):
+    return lax.dot_general(left, right, (((0,), (0,)), ((), ())), preferred_element_type=F32)
+
+
 def along_y(block, both_tables, high_table):
     high, low = halves(block)
     both = dot(both_tables, high)
@@ -133,7 +138,7 @@
     high, low = halves(value)
     narrow = dot_t(high, table[0]) + dot_t(high, table[1]) + dot_t(low, table[0])
     high, low = halves(narrow)
-    wide = dot_t(high, pick) + dot_t(low, pick)
+    wide = dot(high, pick) + dot(low, pick)
     lane = lax.broadcasted_iota(jnp.int32, (FIELDS, 128), 1)
     tiles = [None] * CHUNKS
     for a in range(NK):
@@ -189,10 +194,9 @@
 
 def way_back():
     children = {
-        (0, 0): [(0, 1), (1, 1), (4, 0), (1, 0), (3, 0), (2, 1), (2, 0), (8, 0)],
+        (0, 0): [(0, 1), (1, 1), (4, 0), (1, 0), (3, 1), (2, 1), (3, 0), (2, 0)],
         (0, 1): [(31, 0)],
-        (4, 0): [(5, 0), (5, 1), (6, 0), (7, 0), (6, 1), (4, 1)],
-        (8, 0): [(8, 1), (12, 0), (9, 0), (10, 0), (11, 0)],
+        (8, 0): [(8, 1), (5, 0), (5, 1), (6, 0), (6, 1), (7, 0), (12, 0), (9, 0), (10, 0), (11, 0)],
         (12, 0): [(12, 1), (13, 0), (14, 0), (15, 0)],
         (19, 0): [(19, 1), (16, 0), (17, 0), (18, 0)],
         (23, 0): [(23, 1), (20, 0), (21, 0), (22, 0)],
@@ -231,7 +235,7 @@
     core = gx % 2
     slot = jnp.where(gz == 0, core + flip - 2 * core * flip, core)
     index = 2 * gz + slot
-    is_root = index == 0
+    is_root = functools.reduce(jnp.logical_or, [index == 2 * r for r in ROOTS])
 
     def by_index(table, default):
         value = jnp.int32(default)
@@ -261,12 +265,17 @@
     @pl.when(is_root)
     def _():
         def greet(i, carry):
-            pl.semaphore_signal(barrier, inc=1, device_id=at(y, i // 2, i % 2), device_id_type=MESH)
+            there = (gz + n_z // 4 + i // 2) % n_z
+
+            @pl.when(2 * there + i % 2 != index)
+            def _():
+                pl.semaphore_signal(barrier, inc=1, device_id=at(y, there, i % 2), device_id_type=MESH)
+
             return carry
 
-        lax.fori_loop(1, 2 * n_z, greet, 0)
+        lax.fori_loop(0, 2 * n_z, greet, 0)
         for step in range(1, n_y):
-            pl.semaphore_signal(barrier, inc=1, device_id=at((y + step) % n_y, 0, 0), device_id_type=MESH)
+            pl.semaphore_signal(barrier, inc=1, device_id=at((y + step) % n_y, gz, 0), device_id_type=MESH)
 
     @pl.when(jnp.logical_not(is_root))
     def _():
@@ -302,7 +311,7 @@
             limit = jnp.where(row == f, cutoff[f // 4, f % 4], limit)
         scale[...] = jnp.where(rows[8:16] <= (limit * limit).astype(F32), rate, 0.0)
         for part in range(2):
-            tx_wide[part] = dot(pick[...], tx[part]).astype(BF16)
+            tx_wide[part] = dot_0(pick[...], tx[part]).astype(BF16)
         by[...] = back_y_tables(y_high, y_low)
 
     n_far = 2 * (FAR[1] - FAR[0])
@@ -313,49 +322,54 @@
             src, dst, send_sem.at[which % 3], recv_sem.at[which], device_id=target, device_id_type=MESH
         )
 
-    root = at(y, 0, 0)
+    root = at(y, 16, 0)
+    n_children = by_index({key: len(nodes) for key, nodes in children.items()}, 0)
     busy = [key for key, nodes in children.items() if key == (0, 1) or len(nodes) > 1]
-    is_relay = jnp.logical_and(slot == 0, by_index({key: len(nodes) for key, nodes in children.items()}, 0) == 1)
+    top = [(r, 0) for r in ROOTS]
+    is_relay = jnp.logical_and(slot == 0, n_children == 1)
 
     def pass_on(key):
         for z, child_slot in children[key]:
             remote(total, total, 2, at(y, z, child_slot)).start()
 
+    pl.semaphore_wait(barrier, n_children + jnp.where(is_root, len(ROOTS) + n_y - 2, len(ROOTS)))
+    for r in ROOTS:
+        from_root = (index + 2 * n_z - 2 * r) % (2 * n_z)
+        far = jnp.logical_and(from_root >= 2 * FAR[0], from_root < 2 * FAR[1])
+        after = jnp.where(from_root >= 2 * FAR[1], from_root - n_far, from_root) - 1
+        place = jnp.where(far, n_near + from_root - 2 * FAR[0], after)
+
+        @pl.when(index != 2 * r)
+        def _():
+            pltpu.make_async_remote_copy(
+                pay, got.at[place], send_sem.at[0], recv_sem.at[jnp.where(far, 3, 0)],
+                device_id=at(y, r, 0), device_id_type=MESH,
+            ).start()
+
+    prepare()
+
     @pl.when(jnp.logical_not(is_root))
     def _():
-        pl.semaphore_wait(barrier, 1 + by_index({key: len(nodes) for key, nodes in children.items()}, 0))
-        far = jnp.logical_and(gz >= FAR[0], gz < FAR[1])
-        after = jnp.where(gz >= FAR[1], index - 2 * (FAR[1] - FAR[0]), index)
-        place = jnp.where(far, n_near + index - 2 * FAR[0], after - 1)
-        pltpu.make_async_remote_copy(
-            pay, got.at[place], send_sem.at[0], recv_sem.at[jnp.where(far, 3, 0)],
-            device_id=root, device_id_type=MESH,
-        ).start()
-        prepare()
         remote(total, total, 2, root).wait_recv()
 
-    for key in busy:
-        if key != (0, 0):
-            pl.when(index == 2 * key[0] + key[1])(functools.partial(pass_on, key))
-
-    @pl.when(is_relay)
-    def _():
-        remote(total, total, 2, at(y, gz, 1)).start()
-
     @pl.when(is_root)
     def _():
-        pl.semaphore_wait(barrier, len(children[0, 0]) + n_y - 1)
-        prepare()
         near, far = got.at[pl.ds(0, n_near)], got.at[pl.ds(n_near, n_far)]
         remote(near, near, 0, root).wait_recv()
         first = pay[...] + jnp.sum(near[...], axis=0)
         remote(far, far, 3, root).wait_recv()
         mine_y[...] = first + jnp.sum(far[...], axis=0)
         for step in range(1, n_y):
-            remote(mine_y, got_y.at[step - 1], 1, at((y + step) % n_y, 0, 0)).start()
+            remote(mine_y, got_y.at[step - 1], 1, at((y + step) % n_y, gz, 0)).start()
         remote(got_y, got_y, 1, root).wait_recv()
         total[...] = mine_y[...] + jnp.sum(got_y[...], axis=0)
-        pass_on((0, 0))
+
+    for key in top + [key for key in busy if key not in top]:
+        pl.when(index == 2 * key[0] + key[1])(functools.partial(pass_on, key))
+
+    @pl.when(is_relay)
+    def _():
+        remote(total, total, 2, at(y, gz, 1)).start()
 
     summed = jnp.concatenate([total[c] for c in range(CHUNKS)], axis=1)
     added = back_y(back_x(summed * scale[...], tx_wide[...]), by[...])
@@ -367,13 +381,18 @@
         sent = got.at[pl.ds(0, count)]
         remote(sent, sent, 2, root).wait_send()
 
+    def shares_sent(count):
+        sent = got.at[pl.ds(0, count)]
+        remote(sent, sent, 0, root).wait_send()
+
     @pl.when(is_root)
     def _():
         remote(got_y, got_y, 1, root).wait_send()
+        shares_sent(len(ROOTS) - 1)
 
     @pl.when(jnp.logical_not(is_root))
     def _():
-        remote(pay, pay, 0, root).wait_send()
+        shares_sent(len(ROOTS))
 
     for key in busy:
         pl.when(index == 2 * key[0] + key[1])(functools.partial(pass_on_sent, len(children[key])))
@@ -403,7 +422,7 @@
                 vmem((2, 4, 2 * NK * NK), F32),
                 vmem((2, PAD, 256), BF16),
                 vmem((2, WIDE, 256), BF16),
-                vmem((LANES, WIDE), BF16),
+                vmem((WIDE, LANES), BF16),
                 vmem((NK * NK, LANES), BF16),
                 vmem((4 * FIELDS, LANES), F32),
                 vmem((512, 512), BF16),

time: 42.1 us -> 41.1 us (0.976)
  the two profiles are of different devices: /device:TPU:229 before, /device:TPU:1 now
where the time goes in v4:
time: 41.1 us; the launch traced here: 40.4 us
  Pallas kernels  39.6 us (96%)
  local copies, waits for them, and re-layouts  0.8 us (2%)
    pallas_call x1, Pallas kernels, body(): pl.pallas_call(functools.partial(kernel, n_gx // 2, n_gy), out_shape=jax....  39.6 us

profile of v4, /device:TPU:1, one launch (start us, length us, event | category | flops | bytes accessed | tf_op | source)
XLA Modules:
  0.0 40.4 jit_solution(313062571402338684)
XLA Ops:
  0.0 39.6 %shard_map.100 = f32[2,4,64,256]{3,2,1,0:T(8,128)S(1)} custom-call(s32[2,4]{1,0:T(2,128)} %cutoff_in.1, f32[2,4]{1,0:T(2,128)} %relax_in.1, s32[1,2]{1,0:T(1,128)} %owner_in.1, f32[2,4,64,256]{3,2,1,0:T(8,128)} %state.1, f32[1,2,4,882]{3,2,1,0:T(4,128)} %era.1, bf16[32,2,24,256]{3,2,1,0:T(8,128)(2,1)} %constant.10.clone.tab_y, ...), custom_call_target="tpu_custom_call" | custom-call | tf_op jit(solution)/shard_map/pallas_call | solution.py:412
  39.6 0.8 %copy.12 = f32[2,4,64,256]{3,2,1,0:T(8,128)} copy(f32[2,4,64,256]{3,2,1,0:T(8,128)S(1)} %shard_map.100) | data formatting | bytes 1048576

commit v5 on v4

--- a/solution.py
+++ b/solution.py
@@ -194,7 +194,7 @@
 
 def way_back():
     children = {
-        (0, 0): [(0, 1), (1, 1), (4, 0), (1, 0), (3, 1), (2, 1), (3, 0), (2, 0)],
+        (0, 0): [(1, 1), (1, 0), (4, 0), (2, 1), (2, 0), (0, 1), (3, 1), (3, 0)],
         (0, 1): [(31, 0)],
         (8, 0): [(8, 1), (5, 0), (5, 1), (6, 0), (6, 1), (7, 0), (12, 0), (9, 0), (10, 0), (11, 0)],
         (12, 0): [(12, 1), (13, 0), (14, 0), (15, 0)],
@@ -290,11 +290,9 @@
     copies[1].wait()
     copies[2].wait()
     along = along_y(st[...].reshape(512, 256), y_both, y_high.astype(BF16))
-    copies[3].wait()
-    copies[4].wait()
+    for copy in copies[3:]:
+        copy.wait()
     partial = along_x(along, tx[...], pick[...])
-    for copy in copies[5:]:
-        copy.wait()
     held = folded(jnp.concatenate([er[0], er[1]], axis=0), fold[...], rows[16:24], rows[24:32])
     row = lax.broadcasted_iota(jnp.int32, (8, LANES), 0)
     me = gx * n_z + gz
@@ -359,7 +357,7 @@
         first = pay[...] + jnp.sum(near[...], axis=0)
         remote(far, far, 3, root).wait_recv()
         mine_y[...] = first + jnp.sum(far[...], axis=0)
-        for step in range(1, n_y):
+        for step in sorted(range(1, n_y), key=lambda step: -min(step, n_y - step)):
             remote(mine_y, got_y.at[step - 1], 1, at((y + step) % n_y, gz, 0)).start()
         remote(got_y, got_y, 1, root).wait_recv()
         total[...] = mine_y[...] + jnp.sum(got_y[...], axis=0)

time: 41.1 us -> 40.3 us (0.981)
    pallas_call x1, Pallas kernels: 39.6 us -> 39.2 us  [body(): pl.pallas_call(functools.partial(kernel, n_gx // 2, n_gy), out_shape=jax....]
where the time goes in v5:
time: 40.3 us; the launch traced here: 40 us
  Pallas kernels  39.2 us (97%)
  local copies, waits for them, and re-layouts  0.8 us (2%)
    pallas_call x1, Pallas kernels, body(): pl.pallas_call(functools.partial(kernel, n_gx // 2, n_gy), out_shape=jax....  39.2 us

profile of v5, /device:TPU:1, one launch (start us, length us, event | category | flops | bytes accessed | tf_op | source)
XLA Modules:
  0.0 40.0 jit_solution(13022837732371159292)
XLA Ops:
  0.0 39.2 %shard_map.100 = f32[2,4,64,256]{3,2,1,0:T(8,128)S(1)} custom-call(s32[2,4]{1,0:T(2,128)} %cutoff_in.1, f32[2,4]{1,0:T(2,128)} %relax_in.1, s32[1,2]{1,0:T(1,128)} %owner_in.1, f32[2,4,64,256]{3,2,1,0:T(8,128)} %state.1, f32[1,2,4,882]{3,2,1,0:T(4,128)} %era.1, bf16[32,2,24,256]{3,2,1,0:T(8,128)(2,1)} %constant.10.clone.tab_y, ...), custom_call_target="tpu_custom_call" | custom-call | tf_op jit(solution)/shard_map/pallas_call | solution.py:410
  39.2 0.8 %copy.12 = f32[2,4,64,256]{3,2,1,0:T(8,128)} copy(f32[2,4,64,256]{3,2,1,0:T(8,128)S(1)} %shard_map.100) | data formatting | bytes 1048576

commit v6 on v5

--- a/solution.py
+++ b/solution.py
@@ -134,11 +134,9 @@
     ]
 
 
-def along_x(value, table, pick):
+def along_x(value, high_table, low_table):
     high, low = halves(value)
-    narrow = dot_t(high, table[0]) + dot_t(high, table[1]) + dot_t(low, table[0])
-    high, low = halves(narrow)
-    wide = dot(high, pick) + dot(low, pick)
+    wide = dot(high, high_table) + dot(high, low_table) + dot(low, high_table)
     lane = lax.broadcasted_iota(jnp.int32, (FIELDS, 128), 1)
     tiles = [None] * CHUNKS
     for a in range(NK):
@@ -257,7 +255,7 @@
         pltpu.make_async_copy(cutoff_in, cutoff, in_sem.at[9]),
         pltpu.make_async_copy(relax_in, relax, in_sem.at[10]),
     ]
-    for copy in copies:
+    for copy in [copies[i] for i in (0, 3, 4, 1, 2, 5, 6, 7, 8, 9, 10)]:
         copy.start()
 
     barrier = pltpu.get_barrier_semaphore()
@@ -287,12 +285,16 @@
     copies[0].wait()
     y_high, y_low = blocks(ty[...])
     y_both = jnp.concatenate([y_high, y_low], axis=0).astype(BF16)
+    copies[3].wait()
+    copies[4].wait()
+    x_high = dot_0(tx[0], pick[...]).astype(BF16)
+    x_low = dot_0(tx[1], pick[...]).astype(BF16)
     copies[1].wait()
     copies[2].wait()
     along = along_y(st[...].reshape(512, 256), y_both, y_high.astype(BF16))
-    for copy in copies[3:]:
+    for copy in copies[5:]:
         copy.wait()
-    partial = along_x(along, tx[...], pick[...])
+    partial = along_x(along, x_high, x_low)
     held = folded(jnp.concatenate([er[0], er[1]], axis=0), fold[...], rows[16:24], rows[24:32])
     row = lax.broadcasted_iota(jnp.int32, (8, LANES), 0)
     me = gx * n_z + gz

time: 40.3 us -> 40.3 us (level)
  no operation moved by 1% of the time
where the time goes in v6:
time: 40.3 us; the launch traced here: 40 us
  Pallas kernels  39.2 us (97%)
  local copies, waits for them, and re-layouts  0.8 us (2%)
    pallas_call x1, Pallas kernels, body(): pl.pallas_call(functools.partial(kernel, n_gx // 2, n_gy), out_shape=jax....  39.2 us

profile of v6, /device:TPU:1, one launch (start us, length us, event | category | flops | bytes accessed | tf_op | source)
XLA Modules:
  0.0 40.0 jit_solution(13013716559963480444)
XLA Ops:
  0.0 39.2 %shard_map.100 = f32[2,4,64,256]{3,2,1,0:T(8,128)S(1)} custom-call(s32[2,4]{1,0:T(2,128)} %cutoff_in.1, f32[2,4]{1,0:T(2,128)} %relax_in.1, s32[1,2]{1,0:T(1,128)} %owner_in.1, f32[2,4,64,256]{3,2,1,0:T(8,128)} %state.1, f32[1,2,4,882]{3,2,1,0:T(4,128)} %era.1, bf16[32,2,24,256]{3,2,1,0:T(8,128)(2,1)} %constant.10.clone.tab_y, ...), custom_call_target="tpu_custom_call" | custom-call | tf_op jit(solution)/shard_map/pallas_call | solution.py:412
  39.2 0.8 %copy.12 = f32[2,4,64,256]{3,2,1,0:T(8,128)} copy(f32[2,4,64,256]{3,2,1,0:T(8,128)S(1)} %shard_map.100) | data formatting | bytes 1048576

commit v7 on v5

--- a/solution.py
+++ b/solution.py
@@ -194,13 +194,13 @@
 
 def way_back():
     children = {
-        (0, 0): [(1, 1), (1, 0), (4, 0), (2, 1), (2, 0), (0, 1), (3, 1), (3, 0)],
-        (0, 1): [(31, 0)],
-        (8, 0): [(8, 1), (5, 0), (5, 1), (6, 0), (6, 1), (7, 0), (12, 0), (9, 0), (10, 0), (11, 0)],
+        (0, 0): [(1, 1), (1, 0), (2, 1), (2, 0), (0, 1), (3, 1), (4, 0), (3, 0)],
+        (0, 1): [(23, 0), (31, 0)],
+        (8, 0): [(4, 1), (5, 1), (5, 0), (6, 0), (6, 1), (7, 0), (12, 0), (8, 1), (9, 0), (10, 0), (11, 0)],
         (12, 0): [(12, 1), (13, 0), (14, 0), (15, 0)],
-        (19, 0): [(19, 1), (16, 0), (17, 0), (18, 0)],
-        (23, 0): [(23, 1), (20, 0), (21, 0), (22, 0)],
-        (31, 0): [(31, 1), (19, 0), (23, 0)] + [(z, 0) for z in range(24, 31)],
+        (19, 0): [(16, 0), (17, 0), (18, 0), (19, 1)],
+        (23, 0): [(19, 0), (20, 0), (21, 0), (22, 0), (23, 1)],
+        (31, 0): [(31, 1)] + [(z, 0) for z in range(24, 31)],
     }
     parent = {child: node for node, nodes in children.items() for child in nodes}
     for z in range(1, 32):

time: 40.3 us -> 40.2 us (level)
  no operation moved by 1% of the time
where the time goes in v7:
time: 40.2 us; the launch traced here: 40 us
  Pallas kernels  39.2 us (98%)
  local copies, waits for them, and re-layouts  0.8 us (2%)
    pallas_call x1, Pallas kernels, body(): pl.pallas_call(functools.partial(kernel, n_gx // 2, n_gy), out_shape=jax....  39.2 us

profile of v7, /device:TPU:1, one launch (start us, length us, event | category | flops | bytes accessed | tf_op | source)
XLA Modules:
  0.0 40.0 jit_solution(17400797879793682493)
XLA Ops:
  0.0 39.2 %shard_map.100 = f32[2,4,64,256]{3,2,1,0:T(8,128)S(1)} custom-call(s32[2,4]{1,0:T(2,128)} %cutoff_in.1, f32[2,4]{1,0:T(2,128)} %relax_in.1, s32[1,2]{1,0:T(1,128)} %owner_in.1, f32[2,4,64,256]{3,2,1,0:T(8,128)} %state.1, f32[1,2,4,882]{3,2,1,0:T(4,128)} %era.1, bf16[32,2,24,256]{3,2,1,0:T(8,128)(2,1)} %constant.10.clone.tab_y, ...), custom_call_target="tpu_custom_call" | custom-call | tf_op jit(solution)/shard_map/pallas_call | solution.py:410
  39.2 0.8 %copy.12 = f32[2,4,64,256]{3,2,1,0:T(8,128)} copy(f32[2,4,64,256]{3,2,1,0:T(8,128)S(1)} %shard_map.100) | data formatting | bytes 1048576

commit v8 on v6

--- a/solution.py
+++ b/solution.py
@@ -192,13 +192,13 @@
 
 def way_back():
     children = {
-        (0, 0): [(1, 1), (1, 0), (4, 0), (2, 1), (2, 0), (0, 1), (3, 1), (3, 0)],
-        (0, 1): [(31, 0)],
-        (8, 0): [(8, 1), (5, 0), (5, 1), (6, 0), (6, 1), (7, 0), (12, 0), (9, 0), (10, 0), (11, 0)],
+        (0, 0): [(1, 1), (1, 0), (2, 1), (2, 0), (0, 1), (3, 1), (4, 0), (3, 0)],
+        (0, 1): [(23, 0), (31, 0)],
+        (8, 0): [(4, 1), (5, 1), (5, 0), (6, 0), (6, 1), (7, 0), (12, 0), (8, 1), (9, 0), (10, 0), (11, 0)],
         (12, 0): [(12, 1), (13, 0), (14, 0), (15, 0)],
-        (19, 0): [(19, 1), (16, 0), (17, 0), (18, 0)],
-        (23, 0): [(23, 1), (20, 0), (21, 0), (22, 0)],
-        (31, 0): [(31, 1), (19, 0), (23, 0)] + [(z, 0) for z in range(24, 31)],
+        (19, 0): [(16, 0), (17, 0), (18, 0), (19, 1)],
+        (23, 0): [(19, 0), (20, 0), (21, 0), (22, 0), (23, 1)],
+        (31, 0): [(31, 1)] + [(z, 0) for z in range(24, 31)],
     }
     parent = {child: node for node, nodes in children.items() for child in nodes}
     for z in range(1, 32):

time: 40.3 us -> 40.2 us (level)
  no operation moved by 1% of the time
where the time goes in v8:
time: 40.2 us; the launch traced here: 40 us
  Pallas kernels  39.2 us (98%)
  local copies, waits for them, and re-layouts  0.8 us (2%)
    pallas_call x1, Pallas kernels, body(): pl.pallas_call(functools.partial(kernel, n_gx // 2, n_gy), out_shape=jax....  39.2 us

profile of v8, /device:TPU:1, one launch (start us, length us, event | category | flops | bytes accessed | tf_op | source)
XLA Modules:
  0.0 40.0 jit_solution(2869982709961297164)
XLA Ops:
  0.0 39.2 %shard_map.100 = f32[2,4,64,256]{3,2,1,0:T(8,128)S(1)} custom-call(s32[2,4]{1,0:T(2,128)} %cutoff_in.1, f32[2,4]{1,0:T(2,128)} %relax_in.1, s32[1,2]{1,0:T(1,128)} %owner_in.1, f32[2,4,64,256]{3,2,1,0:T(8,128)} %state.1, f32[1,2,4,882]{3,2,1,0:T(4,128)} %era.1, bf16[32,2,24,256]{3,2,1,0:T(8,128)(2,1)} %constant.10.clone.tab_y, ...), custom_call_target="tpu_custom_call" | custom-call | tf_op jit(solution)/shard_map/pallas_call | solution.py:412
  39.2 0.8 %copy.12 = f32[2,4,64,256]{3,2,1,0:T(8,128)} copy(f32[2,4,64,256]{3,2,1,0:T(8,128)S(1)} %shard_map.100) | data formatting | bytes 1048576
